TPU v7x, 256 devices: a whole 4x4x8 slice. The times are simulated.
256 devices in a mesh: ctx: 16 (over y_lo, x, core), chan: 16 (over z, y_hi).
Axes of the slice: x: 4, y: 4 (y_hi: 2, y_lo: 2; y = y_hi * 2 + y_lo), z: 8, core: 2. Of those that a mesh axis runs over, the one named last changes fastest.
Arguments:
- features: bfloat16 [3, 4096, 4096], P(None, 'ctx', 'chan'), may hold values from -6 to 6
- saved_conv: bfloat16 [4096, 4096], P('ctx', 'chan'), may hold values from -6 to 6
- grad_out: bfloat16 [4096, 4096], P('ctx', 'chan'), may hold values from -6 to 6
- out_weight: bfloat16 [4096, 4096], P('chan'), may hold values from -0.09375 to 0.09375
- in_weight: bfloat16 [3, 4096, 4096], P(None, None, 'chan'), may hold values from -0.09375 to 0.09375
- short_taps: float32 [3, 3, 4096], P(None, None, 'chan'), may hold values from -3.5 to 3.5
- residues: float32 [16, 4096], P(None, 'chan'), may hold values from -1 to 1
- decay_time: float32 [16, 4096], P(None, 'chan'), may hold values from 25 to 20480
Outputs:
- grad_input: bfloat16 [4096, 4096], P('chan', 'ctx')
- grad_residue: float32 [16, 4096], P(None, 'chan')
All inputs are finite; a program needn't handle non-finite values.
Results may differ from a plain program's by a relative error of at most 0.019.
Values may be sent and summed in bfloat16 or wider, within the bound.
A program may use at most 64 MiB of HBM per device.

v0:
```python
import jax
import jax.numpy as jnp
from jax import lax
from jax.sharding import PartitionSpec as P


def passed_along(value, axis, steps):
    count = lax.axis_size(axis)
    leading, last = (max(0, -steps), min(count, count - steps))
    return lax.ppermute(value, axis, [(source, source + steps) for source in range(leading, last)])


def local(features, saved_conv, grad_out, out_weight, in_weight, short_taps, residues, decay_time):
    highest = lax.Precision.HIGHEST
    length = features.shape[1]
    width = features.shape[2]
    poles = residues.shape[0]
    taps = short_taps.shape[1]
    span_rows = 128
    blocks = length // span_rows
    query_act = features[0].astype(jnp.float32)
    key_act = features[1].astype(jnp.float32)
    value_act = features[2].astype(jnp.float32)
    contract = (((1,), (1,)), ((), ()))
    everything = lax.all_gather(grad_out, "chan", axis=1, tiled=True)
    grad_gate = lax.dot_general(
        everything, out_weight, contract, preferred_element_type=jnp.float32
    )
    grad_conv = grad_gate * query_act
    grad_query = grad_gate * saved_conv.astype(jnp.float32)
    product = key_act * value_act
    rate = 1.0 / decay_time
    offset = jnp.arange(span_rows, dtype=jnp.float32)
    falling = jnp.exp(-rate[None] * offset[:, None, None])
    rising = jnp.exp(rate[None] * offset[:, None, None])
    closing = jnp.exp(-rate[None] * (span_rows - offset)[:, None, None])
    weighted = grad_conv.reshape(blocks, span_rows, 1, width) * falling[None]
    upper = (offset[None, :] >= offset[:, None]).astype(jnp.float32)
    tails = jnp.einsum(
        "st,btx->bsx",
        upper,
        weighted.reshape(blocks, span_rows, poles * width),
        precision=highest,
        preferred_element_type=jnp.float32,
    )
    tails = tails.reshape(blocks, span_rows, poles, width)
    starts = tails[:, 0]
    order = jnp.arange(blocks)
    gap = order[None, :] - order[:, None] - 1
    distance = (span_rows * jnp.maximum(gap, 0)).astype(jnp.float32)
    factor = jnp.where(
        gap[:, :, None, None] >= 0, jnp.exp(-rate[None, None] * distance[:, :, None, None]), 0.0
    )
    beyond = jnp.sum(factor * starts[None], axis=1)
    block_span = jnp.exp(-rate * span_rows)
    own_start = starts[0] + block_span * beyond[0]
    device_span = jnp.exp(-rate * length)
    empty = jnp.zeros_like(rate)

    def relay(step, incoming):
        return passed_along(own_start + device_span * incoming, "ctx", -1)

    incoming = lax.fori_loop(0, lax.axis_size("ctx") - 1, relay, empty)
    remain = (blocks - 1 - order).astype(jnp.float32)
    entering = beyond + jnp.exp(-rate[None] * span_rows * remain[:, None, None]) * incoming[None]
    state = tails * rising[None] + closing[None] * entering[:, None]
    grad_product = jnp.sum(residues[None, None] * state, axis=2).reshape(length, width)
    partial_res = jnp.sum(product.reshape(blocks, span_rows, 1, width) * state, axis=(0, 1))
    grad_key = grad_product * value_act
    grad_value = grad_product * key_act
    grad_acts = jnp.stack([grad_query, grad_key, grad_value])
    after = passed_along(grad_acts[:, : taps - 1, :], "ctx", -1)
    extended = jnp.concatenate([grad_acts, after], axis=1)
    filtered = short_taps[:, 0, None, :] * extended[:, 0:length, :]
    for lag in range(1, taps):
        filtered = filtered + short_taps[:, lag, None, :] * extended[:, lag : lag + length, :]
    grad_proj = filtered.astype(jnp.bfloat16)
    grad_input = lax.psum_scatter(
        jnp.einsum("jdc,jtc->dt", in_weight, grad_proj, preferred_element_type=jnp.float32).astype(
            jnp.bfloat16
        ),
        "chan",
        scatter_dimension=0,
        tiled=True,
    )
    grad_residue = lax.psum(partial_res, "ctx") / (length * lax.axis_size("ctx"))
    return (grad_input, grad_residue)


def solution(mesh):
    return jax.shard_map(
        local,
        mesh=mesh,
        in_specs=(
            P(None, "ctx", "chan"),
            P("ctx", "chan"),
            P("ctx", "chan"),
            P("chan", None),
            P(None, None, "chan"),
            P(None, None, "chan"),
            P(None, "chan"),
            P(None, "chan"),
        ),
        out_specs=(P("chan", "ctx"), P(None, "chan")),
        check_vma=False,
    )
```

profile of v0, /device:TPU:2, one launch (start us, length us, event | category | flops | bytes accessed | tf_op | source)
XLA Modules:
  0.0 450.4 jit_solution(12016435469168271515)
XLA Ops:
  9.6 3.1 multiply_exponential_fusion.2
  12.7 2.3 multiply_exponential_fusion
  15.1 83.0 %all-gather.2.cloned.1.call-done = bf16[256,4096]{1,0:T(8,128)(2,1)} async-done(((bf16[256,256]{1,0:T(8,128)(2,1)}), bf16[256,4096]{1,0:T(8,128)(2,1)}) %all-gather.2.cloned.1.call-update) | async-done | bytes 2097168 | tf_op jit(solution)/shard_map/all_gather | solution.py:25
  98.1 2.3 multiply_bitcast_fusion
  102.4 2.1 fusion.12
  107.2 2.8 copy.34
  110.0 2.2 copy.35
  112.4 85.7 %while.10 = (s32[]{:T(128)}, f32[16,256]{1,0:T(8,128)S(1)}, f32[16,256]{1,0:T(8,128)S(1)}, f32[16,256]{1,0:T(8,128)S(1)}, s32[]{:T(128)}) while((s32[]{:T(128)}, f32[16,256]{1,0:T(8,128)S(1)}, f32[16,256]{1,0:T(8,128)S(1)}, f32[16,256]{1,0:T(8,128)S(1)}, s32[]{:T(128)}) %tuple.40), condition=%wide.region_2.3_spmd, body=%wide.region_1.2_spmd.sunk | while | flops 8194 | bytes 131173 | solution.py:63
  112.4 1.9 collective-permute-start
  115.8 3.6 collective-permute-start
  120.8 3.6 collective-permute-start
  125.9 3.6 collective-permute-start
  130.9 3.6 collective-permute-start
  136.0 3.6 collective-permute-start
  141.0 3.6 collective-permute-start
  146.1 3.6 collective-permute-start
  151.1 3.6 collective-permute-start
  156.2 3.6 collective-permute-start
  159.8 2.5 collective-permute-done
  162.3 2.5 collective-permute-start
  164.9 4.6 %collective-permute-done = f32[16,256]{1,0:T(8,128)S(1)} collective-permute-done((f32[16,256]{1,0:T(8,128)S(1)}, f32[16,256]{1,0:T(8,128)S(1)}, u32[]{:S(2)}, u32[]{:S(2)}) %collective-permute-start) | collective-permute-done | bytes 16416 | tf_op jit(solution)/shard_map/while/body/eval_jaxpr/ppermute | solution.py:10
  171.4 5.2 %collective-permute-done = f32[16,256]{1,0:T(8,128)S(1)} collective-permute-done((f32[16,256]{1,0:T(8,128)S(1)}, f32[16,256]{1,0:T(8,128)S(1)}, u32[]{:S(2)}, u32[]{:S(2)}) %collective-permute-start) | collective-permute-done | bytes 16416 | tf_op jit(solution)/shard_map/while/body/eval_jaxpr/ppermute | solution.py:10
  178.6 5.2 %collective-permute-done = f32[16,256]{1,0:T(8,128)S(1)} collective-permute-done((f32[16,256]{1,0:T(8,128)S(1)}, f32[16,256]{1,0:T(8,128)S(1)}, u32[]{:S(2)}, u32[]{:S(2)}) %collective-permute-start) | collective-permute-done | bytes 16416 | tf_op jit(solution)/shard_map/while/body/eval_jaxpr/ppermute | solution.py:10
  185.7 5.2 %collective-permute-done = f32[16,256]{1,0:T(8,128)S(1)} collective-permute-done((f32[16,256]{1,0:T(8,128)S(1)}, f32[16,256]{1,0:T(8,128)S(1)}, u32[]{:S(2)}, u32[]{:S(2)}) %collective-permute-start) | collective-permute-done | bytes 16416 | tf_op jit(solution)/shard_map/while/body/eval_jaxpr/ppermute | solution.py:10
  192.9 5.2 %collective-permute-done = f32[16,256]{1,0:T(8,128)S(1)} collective-permute-done((f32[16,256]{1,0:T(8,128)S(1)}, f32[16,256]{1,0:T(8,128)S(1)}, u32[]{:S(2)}, u32[]{:S(2)}) %collective-permute-start) | collective-permute-done | bytes 16416 | tf_op jit(solution)/shard_map/while/body/eval_jaxpr/ppermute | solution.py:10
  198.2 4.9 %multiply_reduce_fusion = f32[2,128,256]{1,2,0:T(8,128)S(1)} fusion(f32[2,128,16,256]{1,3,2,0:T(8,128)} %bitcast.72, f32[2,16,256]{2,1,0:T(8,128)S(1)} %multiply_add_fusion.2, f32[128,16,256]{0,2,1:T(8,128)} %get-tuple-element.58, f32[128,16,256]{0,2,1:T(8,128)} %get-tuple-element.59, f32[16,256]{1,0:T(8,128)S(1)} %copy-done.5), kind=kLoop, calls=%fused_computation.9 | loop fusion | flops 5177344 | bytes 8699904 | tf_op jit(solution)/shard_map/reduce_sum | solution.py:67
  203.3 1.9 collective-permute-start.1
  205.3 5.2 %collective-permute-done.1 = f32[3,2,256]{2,1,0:T(2,128)S(1)} collective-permute-done((f32[3,2,256]{2,1,0:T(2,128)S(1)}, f32[3,2,256]{2,1,0:T(2,128)S(1)}, u32[]{:S(2)}, u32[]{:S(2)}) %collective-permute-start.1) | collective-permute-done | bytes 6176 | tf_op jit(solution)/shard_map/ppermute | solution.py:10
  210.6 6.0 %fusion.1 = bf16[4096,256]{0,1:T(8,128)(2,1)} fusion(bf16[3,4096,256]{2,1,0:T(8,128)(2,1)} %param.14, f32[3,258,256]{2,1,0:T(8,128)S(1)} %pad_maximum_fusion, f32[3,256]{1,0:T(4,128)S(1)} %get-tuple-element.60, f32[3,256]{1,0:T(4,128)S(1)} %get-tuple-element.61, f32[3,256]{1,0:T(4,128)S(1)} %bitcast.84, f32[1,256,256]{2,1,0:T(8,128)S(1)} %get-tuple-element.42, ...), kind=kOutput, calls=%fused_computation.3 | convolution fusion | flops 1613234176 | bytes 10760192 | tf_op jit(solution)/shard_map/jdc,jtc->dt/dot_general | solution.py:79
  218.7 4.4 fusion.2
  223.1 63.4 %psum.7 = f32[16,256]{1,0:T(8,128)S(1)} all-reduce(f32[16,256]{1,0:T(8,128)S(1)} %reduce_sum.35), channel_id=1, replica_groups=mesh['ctx'=16,'chan'=16] {'ctx'}, use_global_device_ids=true, to_apply=%region_6.7 | all-reduce | flops 4096 | bytes 32768 | tf_op jit(solution)/shard_map/psum | solution.py:86
  287.1 154.8 %reduce-scatter.2.cloned.1.call-done = bf16[256,256]{0,1:T(8,128)(2,1)} async-done(((bf16[4096,256]{0,1:T(8,128)(2,1)}), bf16[256,256]{0,1:T(8,128)(2,1)}) %reduce-scatter.2.cloned.1.call-update) | async-done | bytes 131088 | tf_op jit(solution)/shard_map/reduce_scatter | solution.py:78
  (75 shorter events, 32.3 us)
Async XLA Ops:
  7.2 90.9 %copy-start = (bf16[256,4096]{1,0:T(8,128)(2,1)S(1)}, bf16[256,4096]{1,0:T(8,128)(2,1)}, u32[]{:S(2)}) copy-start(bf16[256,4096]{1,0:T(8,128)(2,1)} %param.13) | copy-start | bytes 6291460
  7.2 90.9 %all-gather.2.cloned.1.call-start = ((), (), s32[]{:S(2)}) async-start(), calls=%async_computation.1 | async-start | bytes 2228224 | tf_op jit(solution)/shard_map/all_gather | solution.py:25
  7.9 434.0 %reduce-scatter.2.cloned.1.call-start = ((), (), s32[]{:S(2)}) async-start(), calls=%async_computation.2 | async-start | bytes 2228224 | tf_op jit(solution)/shard_map/reduce_scatter | solution.py:78
  12.7 85.3 %copy-start.2 = (bf16[3,256,256]{2,1,0:T(8,128)(2,1)S(1)}, bf16[3,256,256]{2,1,0:T(8,128)(2,1)}, u32[]{:S(2)}) copy-start(bf16[3,256,256]{2,1,0:T(8,128)(2,1)} %param.10) | copy-start | bytes 1179652
  12.7 85.3 %copy-start.3 = (bf16[256,256]{1,0:T(8,128)(2,1)S(1)}, bf16[256,256]{1,0:T(8,128)(2,1)}, u32[]{:S(2)}) copy-start(bf16[256,256]{1,0:T(8,128)(2,1)} %param.11) | copy-start | bytes 393220
  104.5 2.6 copy-start.1
  110.0 2.3 copy-start.4
  110.0 88.2 %copy-start.5 = (f32[16,256]{1,0:T(8,128)S(1)}, f32[16,256]{1,0:T(8,128)}, u32[]{:S(2)}) copy-start(f32[16,256]{1,0:T(8,128)} %param.16) | copy-start | bytes 49156
  112.4 3.4 collective-permute-start
  115.8 5.0 %collective-permute-start = (f32[16,256]{1,0:T(8,128)S(1)}, f32[16,256]{1,0:T(8,128)S(1)}, u32[]{:S(2)}, u32[]{:S(2)}) collective-permute-start(f32[16,256]{1,0:T(8,128)S(1)} %multiply_add_fusion.4), channel_id=1, source_target_pairs={{16,0},{32,16},{48,32},{64,48},{80,64},{96,80},{112,96},{128,112},... | collective-permute-start | bytes 49160 | tf_op jit(solution)/shard_map/while/body/eval_jaxpr/ppermute | solution.py:10
  120.8 5.0 %collective-permute-start = (f32[16,256]{1,0:T(8,128)S(1)}, f32[16,256]{1,0:T(8,128)S(1)}, u32[]{:S(2)}, u32[]{:S(2)}) collective-permute-start(f32[16,256]{1,0:T(8,128)S(1)} %multiply_add_fusion.4), channel_id=1, source_target_pairs={{16,0},{32,16},{48,32},{64,48},{80,64},{96,80},{112,96},{128,112},... | collective-permute-start | bytes 49160 | tf_op jit(solution)/shard_map/while/body/eval_jaxpr/ppermute | solution.py:10
  125.9 5.0 %collective-permute-start = (f32[16,256]{1,0:T(8,128)S(1)}, f32[16,256]{1,0:T(8,128)S(1)}, u32[]{:S(2)}, u32[]{:S(2)}) collective-permute-start(f32[16,256]{1,0:T(8,128)S(1)} %multiply_add_fusion.4), channel_id=1, source_target_pairs={{16,0},{32,16},{48,32},{64,48},{80,64},{96,80},{112,96},{128,112},... | collective-permute-start | bytes 49160 | tf_op jit(solution)/shard_map/while/body/eval_jaxpr/ppermute | solution.py:10
  130.9 5.0 %collective-permute-start = (f32[16,256]{1,0:T(8,128)S(1)}, f32[16,256]{1,0:T(8,128)S(1)}, u32[]{:S(2)}, u32[]{:S(2)}) collective-permute-start(f32[16,256]{1,0:T(8,128)S(1)} %multiply_add_fusion.4), channel_id=1, source_target_pairs={{16,0},{32,16},{48,32},{64,48},{80,64},{96,80},{112,96},{128,112},... | collective-permute-start | bytes 49160 | tf_op jit(solution)/shard_map/while/body/eval_jaxpr/ppermute | solution.py:10
  136.0 5.0 %collective-permute-start = (f32[16,256]{1,0:T(8,128)S(1)}, f32[16,256]{1,0:T(8,128)S(1)}, u32[]{:S(2)}, u32[]{:S(2)}) collective-permute-start(f32[16,256]{1,0:T(8,128)S(1)} %multiply_add_fusion.4), channel_id=1, source_target_pairs={{16,0},{32,16},{48,32},{64,48},{80,64},{96,80},{112,96},{128,112},... | collective-permute-start | bytes 49160 | tf_op jit(solution)/shard_map/while/body/eval_jaxpr/ppermute | solution.py:10
  141.0 5.0 %collective-permute-start = (f32[16,256]{1,0:T(8,128)S(1)}, f32[16,256]{1,0:T(8,128)S(1)}, u32[]{:S(2)}, u32[]{:S(2)}) collective-permute-start(f32[16,256]{1,0:T(8,128)S(1)} %multiply_add_fusion.4), channel_id=1, source_target_pairs={{16,0},{32,16},{48,32},{64,48},{80,64},{96,80},{112,96},{128,112},... | collective-permute-start | bytes 49160 | tf_op jit(solution)/shard_map/while/body/eval_jaxpr/ppermute | solution.py:10
  146.1 5.0 %collective-permute-start = (f32[16,256]{1,0:T(8,128)S(1)}, f32[16,256]{1,0:T(8,128)S(1)}, u32[]{:S(2)}, u32[]{:S(2)}) collective-permute-start(f32[16,256]{1,0:T(8,128)S(1)} %multiply_add_fusion.4), channel_id=1, source_target_pairs={{16,0},{32,16},{48,32},{64,48},{80,64},{96,80},{112,96},{128,112},... | collective-permute-start | bytes 49160 | tf_op jit(solution)/shard_map/while/body/eval_jaxpr/ppermute | solution.py:10
  151.1 5.0 %collective-permute-start = (f32[16,256]{1,0:T(8,128)S(1)}, f32[16,256]{1,0:T(8,128)S(1)}, u32[]{:S(2)}, u32[]{:S(2)}) collective-permute-start(f32[16,256]{1,0:T(8,128)S(1)} %multiply_add_fusion.4), channel_id=1, source_target_pairs={{16,0},{32,16},{48,32},{64,48},{80,64},{96,80},{112,96},{128,112},... | collective-permute-start | bytes 49160 | tf_op jit(solution)/shard_map/while/body/eval_jaxpr/ppermute | solution.py:10
  156.2 6.1 %collective-permute-start = (f32[16,256]{1,0:T(8,128)S(1)}, f32[16,256]{1,0:T(8,128)S(1)}, u32[]{:S(2)}, u32[]{:S(2)}) collective-permute-start(f32[16,256]{1,0:T(8,128)S(1)} %multiply_add_fusion.4), channel_id=1, source_target_pairs={{16,0},{32,16},{48,32},{64,48},{80,64},{96,80},{112,96},{128,112},... | collective-permute-start | bytes 49160 | tf_op jit(solution)/shard_map/while/body/eval_jaxpr/ppermute | solution.py:10
  162.3 7.2 %collective-permute-start = (f32[16,256]{1,0:T(8,128)S(1)}, f32[16,256]{1,0:T(8,128)S(1)}, u32[]{:S(2)}, u32[]{:S(2)}) collective-permute-start(f32[16,256]{1,0:T(8,128)S(1)} %multiply_add_fusion.4), channel_id=1, source_target_pairs={{16,0},{32,16},{48,32},{64,48},{80,64},{96,80},{112,96},{128,112},... | collective-permute-start | bytes 49160 | tf_op jit(solution)/shard_map/while/body/eval_jaxpr/ppermute | solution.py:10
  169.5 7.2 %collective-permute-start = (f32[16,256]{1,0:T(8,128)S(1)}, f32[16,256]{1,0:T(8,128)S(1)}, u32[]{:S(2)}, u32[]{:S(2)}) collective-permute-start(f32[16,256]{1,0:T(8,128)S(1)} %multiply_add_fusion.4), channel_id=1, source_target_pairs={{16,0},{32,16},{48,32},{64,48},{80,64},{96,80},{112,96},{128,112},... | collective-permute-start | bytes 49160 | tf_op jit(solution)/shard_map/while/body/eval_jaxpr/ppermute | solution.py:10
  176.6 7.2 %collective-permute-start = (f32[16,256]{1,0:T(8,128)S(1)}, f32[16,256]{1,0:T(8,128)S(1)}, u32[]{:S(2)}, u32[]{:S(2)}) collective-permute-start(f32[16,256]{1,0:T(8,128)S(1)} %multiply_add_fusion.4), channel_id=1, source_target_pairs={{16,0},{32,16},{48,32},{64,48},{80,64},{96,80},{112,96},{128,112},... | collective-permute-start | bytes 49160 | tf_op jit(solution)/shard_map/while/body/eval_jaxpr/ppermute | solution.py:10
  183.8 7.2 %collective-permute-start = (f32[16,256]{1,0:T(8,128)S(1)}, f32[16,256]{1,0:T(8,128)S(1)}, u32[]{:S(2)}, u32[]{:S(2)}) collective-permute-start(f32[16,256]{1,0:T(8,128)S(1)} %multiply_add_fusion.4), channel_id=1, source_target_pairs={{16,0},{32,16},{48,32},{64,48},{80,64},{96,80},{112,96},{128,112},... | collective-permute-start | bytes 49160 | tf_op jit(solution)/shard_map/while/body/eval_jaxpr/ppermute | solution.py:10
  191.0 7.2 %collective-permute-start = (f32[16,256]{1,0:T(8,128)S(1)}, f32[16,256]{1,0:T(8,128)S(1)}, u32[]{:S(2)}, u32[]{:S(2)}) collective-permute-start(f32[16,256]{1,0:T(8,128)S(1)} %multiply_add_fusion.4), channel_id=1, source_target_pairs={{16,0},{32,16},{48,32},{64,48},{80,64},{96,80},{112,96},{128,112},... | collective-permute-start | bytes 49160 | tf_op jit(solution)/shard_map/while/body/eval_jaxpr/ppermute | solution.py:10
  203.3 7.2 %collective-permute-start.1 = (f32[3,2,256]{2,1,0:T(2,128)S(1)}, f32[3,2,256]{2,1,0:T(2,128)S(1)}, u32[]{:S(2)}, u32[]{:S(2)}) collective-permute-start(f32[3,2,256]{2,1,0:T(2,128)S(1)} %slice.53), channel_id=1, source_target_pairs={{16,0},{32,16},{48,32},{64,48},{80,64},{96,80},{112,96},{128,112},... | collective-permute-start | bytes 18440 | tf_op jit(solution)/shard_map/ppermute | solution.py:10
Sparse Core Ops, SparseCore 0:
  10.5 87.5 all-gather.1
  216.7 225.1 reduce-scatter.1
where the time goes:
time: 451 us; the launch traced here: 450 us
  waiting for transfers between devices  285 us (63%)
  blocking collectives  63.4 us (14%)
  starting transfers between devices  46.6 us (10%)
  other arithmetic  20.2 us (4%)
  between operations  14.3 us (3%)
  local copies, waits for them, and re-layouts  10.6 us (2%)
  matrix products  10.5 us (2%)
    reduce_scatter x1, waiting for transfers between devices, local(): lax.psum_scatter(jnp.einsum('jdc,jtc->dt', in_weight, grad_proj, preferre...  155 us
    all_gather x1, waiting for transfers between devices, local(): everything = lax.all_gather(grad_out, 'chan', axis=1, tiled=True)  83 us
    psum x1, blocking collectives, local(): lax.psum(partial_res, 'ctx') / (length * lax.axis_size('ctx'))  63.4 us
    ppermute x16, starting transfers between devices, passed_along(): lax.ppermute(value, axis, [(source, source + steps) for source in range(l...  46.6 us
    ppermute x16, waiting for transfers between devices, passed_along(): lax.ppermute(value, axis, [(source, source + steps) for source in range(l...  46 us
  transfers between devices with their start and end apart: 18, of which 18 were waited for; matrix products, arithmetic and copies ran while one was open for 3% of the time, Pallas kernels for 0%

commit v1 on v0

--- a/solution.py
+++ b/solution.py
@@ -1,7 +1,23 @@
+import functools
 import jax
 import jax.numpy as jnp
 from jax import lax
 from jax.sharding import PartitionSpec as P
+
+
+def note_pages_on(u, pos_dim):
+    return jnp.concatenate(
+        jax.lax.all_to_all(
+            jnp.stack(jax.lax.axis_size("chan") * [u]),
+            axis_name="chan",
+            split_axis=0,
+            concat_axis=0,
+        ),
+        axis=pos_dim,
+    )
+
+
+solve_column = functools.partial(note_pages_on, pos_dim=1)
 
 
 def passed_along(value, axis, steps):
@@ -22,7 +38,7 @@
     key_act = features[1].astype(jnp.float32)
     value_act = features[2].astype(jnp.float32)
     contract = (((1,), (1,)), ((), ()))
-    everything = lax.all_gather(grad_out, "chan", axis=1, tiled=True)
+    everything = solve_column(grad_out)
     grad_gate = lax.dot_general(
         everything, out_weight, contract, preferred_element_type=jnp.float32
     )

time: 451 us -> 427 us (0.947)
  waiting for transfers between devices: 285 us -> 248 us
  starting transfers between devices: 46.6 us -> 57.4 us
    all_gather x1 -> x0, waiting for transfers between devices: 83 us -> none  [local(): everything = lax.all_gather(grad_out, 'chan', axis=1, tiled=True)]
    all_to_all x0 -> x1, waiting for transfers between devices: none -> 46.4 us  [note_pages_on(): jax.lax.all_to_all(jnp.stack(jax.lax.axis_size('chan') * [u]), axis_name=...]
    all_to_all x0 -> x1, starting transfers between devices: none -> 11.4 us  [note_pages_on(): jax.lax.all_to_all(jnp.stack(jax.lax.axis_size('chan') * [u]), axis_name=...]
where the time goes in v1:
time: 427 us
  waiting for transfers between devices  248 us (58%)
  blocking collectives  63.7 us (15%)
  starting transfers between devices  57.4 us (13%)
  other arithmetic  19.5 us (5%)
  between operations  14.3 us (3%)
  local copies, waits for them, and re-layouts  12.5 us (3%)
  matrix products  10.5 us (2%)
    reduce_scatter x1, waiting for transfers between devices, local(): lax.psum_scatter(jnp.einsum('jdc,jtc->dt', in_weight, grad_proj, preferre...  155 us
    psum x1, blocking collectives, local(): lax.psum(partial_res, 'ctx') / (length * lax.axis_size('ctx'))  63.7 us
    ppermute x16, waiting for transfers between devices, passed_along(): lax.ppermute(value, axis, [(source, source + steps) for source in range(l...  47.3 us
    all_to_all x1, waiting for transfers between devices, note_pages_on(): jax.lax.all_to_all(jnp.stack(jax.lax.axis_size('chan') * [u]), axis_name=...  46.4 us
    ppermute x16, starting transfers between devices, passed_along(): lax.ppermute(value, axis, [(source, source + steps) for source in range(l...  45.9 us
    all_to_all x1, starting transfers between devices, note_pages_on(): jax.lax.all_to_all(jnp.stack(jax.lax.axis_size('chan') * [u]), axis_name=...  11.4 us
    unnamed x25, local copies, waits for them, and re-layouts  8.98 us
  transfers between devices with their start and end apart: 18, of which 18 were waited for; matrix products, arithmetic and copies ran while one was open for 3% of the time, Pallas kernels for 0%

profile of v1, /device:TPU:2, one launch (start us, length us, event | category | flops | bytes accessed | tf_op | source)
XLA Modules:
  0.0 426.5 jit_solution(17996620497709196146)
XLA Ops:
  9.9 11.4 %all-to-all-start = ((bf16[16,256,256]{1,2,0:T(8,128)(2,1)}), bf16[16,256,256]{1,2,0:T(8,128)(2,1)}, u32[]{:S(2)}, u32[]{:S(2)}) async-start(bf16[16,256,256]{1,2,0:T(8,128)(2,1)} %stack.6), calls=%async_computation | async-start | bytes 4194304 | tf_op jit(solution)/shard_map/all_to_all | solution.py:10
  21.4 3.1 multiply_exponential_fusion.2
  24.5 2.4 multiply_exponential_fusion
  26.9 46.4 %all-to-all-done = bf16[16,256,256]{1,2,0:T(8,128)(2,1)} async-done(((bf16[16,256,256]{1,2,0:T(8,128)(2,1)}), bf16[16,256,256]{1,2,0:T(8,128)(2,1)}, u32[]{:S(2)}, u32[]{:S(2)}) %all-to-all-start) | async-done | bytes 2097184 | tf_op jit(solution)/shard_map/all_to_all | solution.py:10
  73.3 2.3 multiply_bitcast_fusion
  77.7 2.1 fusion.12
  82.4 2.8 copy.37
  85.3 2.2 copy.38
  87.6 86.4 %while.10 = (s32[]{:T(128)}, f32[16,256]{1,0:T(8,128)S(1)}, f32[16,256]{1,0:T(8,128)S(1)}, f32[16,256]{1,0:T(8,128)S(1)}, s32[]{:T(128)}) while((s32[]{:T(128)}, f32[16,256]{1,0:T(8,128)S(1)}, f32[16,256]{1,0:T(8,128)S(1)}, f32[16,256]{1,0:T(8,128)S(1)}, s32[]{:T(128)}) %tuple.40), condition=%wide.region_2.3_spmd, body=%wide.region_1.2_spmd.sunk | while | flops 8194 | bytes 131173 | solution.py:79
  87.6 1.9 collective-permute-start
  91.0 3.6 collective-permute-start
  96.1 3.6 collective-permute-start
  101.1 3.6 collective-permute-start
  106.2 3.6 collective-permute-start
  111.2 3.6 collective-permute-start
  116.3 3.6 collective-permute-start
  121.3 3.6 collective-permute-start
  126.4 3.6 collective-permute-start
  131.4 3.6 collective-permute-start
  135.1 3.2 collective-permute-done
  140.2 5.2 %collective-permute-done = f32[16,256]{1,0:T(8,128)S(1)} collective-permute-done((f32[16,256]{1,0:T(8,128)S(1)}, f32[16,256]{1,0:T(8,128)S(1)}, u32[]{:S(2)}, u32[]{:S(2)}) %collective-permute-start) | collective-permute-done | bytes 16416 | tf_op jit(solution)/shard_map/while/body/eval_jaxpr/ppermute | solution.py:26
  147.3 5.2 %collective-permute-done = f32[16,256]{1,0:T(8,128)S(1)} collective-permute-done((f32[16,256]{1,0:T(8,128)S(1)}, f32[16,256]{1,0:T(8,128)S(1)}, u32[]{:S(2)}, u32[]{:S(2)}) %collective-permute-start) | collective-permute-done | bytes 16416 | tf_op jit(solution)/shard_map/while/body/eval_jaxpr/ppermute | solution.py:26
  154.5 5.2 %collective-permute-done = f32[16,256]{1,0:T(8,128)S(1)} collective-permute-done((f32[16,256]{1,0:T(8,128)S(1)}, f32[16,256]{1,0:T(8,128)S(1)}, u32[]{:S(2)}, u32[]{:S(2)}) %collective-permute-start) | collective-permute-done | bytes 16416 | tf_op jit(solution)/shard_map/while/body/eval_jaxpr/ppermute | solution.py:26
  161.6 5.2 %collective-permute-done = f32[16,256]{1,0:T(8,128)S(1)} collective-permute-done((f32[16,256]{1,0:T(8,128)S(1)}, f32[16,256]{1,0:T(8,128)S(1)}, u32[]{:S(2)}, u32[]{:S(2)}) %collective-permute-start) | collective-permute-done | bytes 16416 | tf_op jit(solution)/shard_map/while/body/eval_jaxpr/ppermute | solution.py:26
  168.8 5.2 %collective-permute-done = f32[16,256]{1,0:T(8,128)S(1)} collective-permute-done((f32[16,256]{1,0:T(8,128)S(1)}, f32[16,256]{1,0:T(8,128)S(1)}, u32[]{:S(2)}, u32[]{:S(2)}) %collective-permute-start) | collective-permute-done | bytes 16416 | tf_op jit(solution)/shard_map/while/body/eval_jaxpr/ppermute | solution.py:26
  174.1 4.9 %multiply_reduce_fusion = f32[2,128,256]{1,2,0:T(8,128)S(1)} fusion(f32[2,128,16,256]{1,3,2,0:T(8,128)} %bitcast.75, f32[2,16,256]{2,1,0:T(8,128)S(1)} %multiply_add_fusion.2, f32[128,16,256]{0,2,1:T(8,128)} %get-tuple-element.58, f32[128,16,256]{0,2,1:T(8,128)} %get-tuple-element.59, f32[16,256]{1,0:T(8,128)S(1)} %copy-done.5), kind=kLoop, calls=%fused_computation.9 | loop fusion | flops 5177344 | bytes 8699904 | tf_op jit(solution)/shard_map/reduce_sum | solution.py:83
  179.3 1.9 collective-permute-start.1
  181.2 5.2 %collective-permute-done.1 = f32[3,2,256]{2,1,0:T(2,128)S(1)} collective-permute-done((f32[3,2,256]{2,1,0:T(2,128)S(1)}, f32[3,2,256]{2,1,0:T(2,128)S(1)}, u32[]{:S(2)}, u32[]{:S(2)}) %collective-permute-start.1) | collective-permute-done | bytes 6176 | tf_op jit(solution)/shard_map/ppermute | solution.py:26
  186.5 6.0 %fusion.1 = bf16[4096,256]{0,1:T(8,128)(2,1)} fusion(bf16[3,4096,256]{2,1,0:T(8,128)(2,1)} %param.14, f32[3,258,256]{2,1,0:T(8,128)S(1)} %pad_maximum_fusion, f32[3,256]{1,0:T(4,128)S(1)} %get-tuple-element.60, f32[3,256]{1,0:T(4,128)S(1)} %get-tuple-element.61, f32[3,256]{1,0:T(4,128)S(1)} %bitcast.87, f32[1,256,256]{2,1,0:T(8,128)S(1)} %get-tuple-element.42, ...), kind=kOutput, calls=%fused_computation.3 | convolution fusion | flops 1613234176 | bytes 10760192 | tf_op jit(solution)/shard_map/jdc,jtc->dt/dot_general | solution.py:95
  194.6 4.4 %fusion.2 = f32[4096]{0:T(1024)S(1)} fusion(f32[2,4096,128]{2,1,0:T(8,128)} %copy-done.1, f32[2,4096]{1,0:T(2,128)S(1)} %multiply_add_fusion.1, f32[128,4096]{0,1:T(8,128)} %get-tuple-element.53, f32[128,4096]{0,1:T(8,128)} %multiply_exponential_fusion.1, f32[2,128,256]{1,2,0:T(8,128)S(1)} %copy.32), kind=kLoop, calls=%fused_computation.5 | loop fusion | flops 5238784 | bytes 8699904 | tf_op jit(solution)/shard_map/reduce_sum | solution.py:84
  199.0 63.7 %psum.7 = f32[16,256]{1,0:T(8,128)S(1)} all-reduce(f32[16,256]{1,0:T(8,128)S(1)} %reduce_sum.35), channel_id=1, replica_groups=mesh['ctx'=16,'chan'=16] {'ctx'}, use_global_device_ids=true, to_apply=%region_6.7 | all-reduce | flops 4096 | bytes 32768 | tf_op jit(solution)/shard_map/psum | solution.py:102
  263.3 154.7 %reduce-scatter.2.cloned.1.call-done = bf16[256,256]{0,1:T(8,128)(2,1)} async-done(((bf16[4096,256]{0,1:T(8,128)(2,1)}), bf16[256,256]{0,1:T(8,128)(2,1)}) %reduce-scatter.2.cloned.1.call-update) | async-done | bytes 131088 | tf_op jit(solution)/shard_map/reduce_scatter | solution.py:94
  (78 shorter events, 34.6 us)
Async XLA Ops:
  7.2 66.1 %copy-start = (bf16[256,4096]{1,0:T(8,128)(2,1)S(1)}, bf16[256,4096]{1,0:T(8,128)(2,1)}, u32[]{:S(2)}) copy-start(bf16[256,4096]{1,0:T(8,128)(2,1)} %param.13) | copy-start | bytes 6291460
  9.8 11.4 %copy-start.4 = (f32[16,256]{1,0:T(8,128)S(1)}, f32[16,256]{1,0:T(8,128)}, u32[]{:S(2)}) copy-start(f32[16,256]{1,0:T(8,128)} %param.17) | copy-start | bytes 49156
  9.9 11.5 %copy-start.6 = (f32[3,3,256]{2,1,0:T(4,128)S(1)}, f32[3,3,256]{2,1,0:T(4,128)}, u32[]{:S(2)}) copy-start(f32[3,3,256]{2,1,0:T(4,128)} %param.15) | copy-start | bytes 27652
  9.9 63.5 %all-to-all-start = ((bf16[16,256,256]{1,2,0:T(8,128)(2,1)}), bf16[16,256,256]{1,2,0:T(8,128)(2,1)}, u32[]{:S(2)}, u32[]{:S(2)}) async-start(bf16[16,256,256]{1,2,0:T(8,128)(2,1)} %stack.6), calls=%async_computation | async-start | bytes 4194304 | tf_op jit(solution)/shard_map/all_to_all | solution.py:10
  21.2 396.8 %reduce-scatter.2.cloned.1.call-start = ((), (), s32[]{:S(2)}) async-start(), calls=%async_computation.2 | async-start | bytes 2228224 | tf_op jit(solution)/shard_map/reduce_scatter | solution.py:94
  24.5 48.8 %copy-start.2 = (bf16[3,256,256]{2,1,0:T(8,128)(2,1)S(1)}, bf16[3,256,256]{2,1,0:T(8,128)(2,1)}, u32[]{:S(2)}) copy-start(bf16[3,256,256]{2,1,0:T(8,128)(2,1)} %param.10) | copy-start | bytes 1179652
  24.5 48.8 %copy-start.3 = (bf16[256,256]{1,0:T(8,128)(2,1)S(1)}, bf16[256,256]{1,0:T(8,128)(2,1)}, u32[]{:S(2)}) copy-start(bf16[256,256]{1,0:T(8,128)(2,1)} %param.11) | copy-start | bytes 393220
  79.8 2.6 copy-start.1
  85.3 88.9 %copy-start.5 = (f32[16,256]{1,0:T(8,128)S(1)}, f32[16,256]{1,0:T(8,128)}, u32[]{:S(2)}) copy-start(f32[16,256]{1,0:T(8,128)} %param.16) | copy-start | bytes 49156
  87.6 3.4 collective-permute-start
  91.0 5.0 %collective-permute-start = (f32[16,256]{1,0:T(8,128)S(1)}, f32[16,256]{1,0:T(8,128)S(1)}, u32[]{:S(2)}, u32[]{:S(2)}) collective-permute-start(f32[16,256]{1,0:T(8,128)S(1)} %multiply_add_fusion.4), channel_id=1, source_target_pairs={{16,0},{32,16},{48,32},{64,48},{80,64},{96,80},{112,96},{128,112},... | collective-permute-start | bytes 49160 | tf_op jit(solution)/shard_map/while/body/eval_jaxpr/ppermute | solution.py:26
  96.1 5.0 %collective-permute-start = (f32[16,256]{1,0:T(8,128)S(1)}, f32[16,256]{1,0:T(8,128)S(1)}, u32[]{:S(2)}, u32[]{:S(2)}) collective-permute-start(f32[16,256]{1,0:T(8,128)S(1)} %multiply_add_fusion.4), channel_id=1, source_target_pairs={{16,0},{32,16},{48,32},{64,48},{80,64},{96,80},{112,96},{128,112},... | collective-permute-start | bytes 49160 | tf_op jit(solution)/shard_map/while/body/eval_jaxpr/ppermute | solution.py:26
  101.1 5.0 %collective-permute-start = (f32[16,256]{1,0:T(8,128)S(1)}, f32[16,256]{1,0:T(8,128)S(1)}, u32[]{:S(2)}, u32[]{:S(2)}) collective-permute-start(f32[16,256]{1,0:T(8,128)S(1)} %multiply_add_fusion.4), channel_id=1, source_target_pairs={{16,0},{32,16},{48,32},{64,48},{80,64},{96,80},{112,96},{128,112},... | collective-permute-start | bytes 49160 | tf_op jit(solution)/shard_map/while/body/eval_jaxpr/ppermute | solution.py:26
  106.2 5.0 %collective-permute-start = (f32[16,256]{1,0:T(8,128)S(1)}, f32[16,256]{1,0:T(8,128)S(1)}, u32[]{:S(2)}, u32[]{:S(2)}) collective-permute-start(f32[16,256]{1,0:T(8,128)S(1)} %multiply_add_fusion.4), channel_id=1, source_target_pairs={{16,0},{32,16},{48,32},{64,48},{80,64},{96,80},{112,96},{128,112},... | collective-permute-start | bytes 49160 | tf_op jit(solution)/shard_map/while/body/eval_jaxpr/ppermute | solution.py:26
  111.2 5.0 %collective-permute-start = (f32[16,256]{1,0:T(8,128)S(1)}, f32[16,256]{1,0:T(8,128)S(1)}, u32[]{:S(2)}, u32[]{:S(2)}) collective-permute-start(f32[16,256]{1,0:T(8,128)S(1)} %multiply_add_fusion.4), channel_id=1, source_target_pairs={{16,0},{32,16},{48,32},{64,48},{80,64},{96,80},{112,96},{128,112},... | collective-permute-start | bytes 49160 | tf_op jit(solution)/shard_map/while/body/eval_jaxpr/ppermute | solution.py:26
  116.3 5.0 %collective-permute-start = (f32[16,256]{1,0:T(8,128)S(1)}, f32[16,256]{1,0:T(8,128)S(1)}, u32[]{:S(2)}, u32[]{:S(2)}) collective-permute-start(f32[16,256]{1,0:T(8,128)S(1)} %multiply_add_fusion.4), channel_id=1, source_target_pairs={{16,0},{32,16},{48,32},{64,48},{80,64},{96,80},{112,96},{128,112},... | collective-permute-start | bytes 49160 | tf_op jit(solution)/shard_map/while/body/eval_jaxpr/ppermute | solution.py:26
  121.3 5.0 %collective-permute-start = (f32[16,256]{1,0:T(8,128)S(1)}, f32[16,256]{1,0:T(8,128)S(1)}, u32[]{:S(2)}, u32[]{:S(2)}) collective-permute-start(f32[16,256]{1,0:T(8,128)S(1)} %multiply_add_fusion.4), channel_id=1, source_target_pairs={{16,0},{32,16},{48,32},{64,48},{80,64},{96,80},{112,96},{128,112},... | collective-permute-start | bytes 49160 | tf_op jit(solution)/shard_map/while/body/eval_jaxpr/ppermute | solution.py:26
  126.4 5.0 %collective-permute-start = (f32[16,256]{1,0:T(8,128)S(1)}, f32[16,256]{1,0:T(8,128)S(1)}, u32[]{:S(2)}, u32[]{:S(2)}) collective-permute-start(f32[16,256]{1,0:T(8,128)S(1)} %multiply_add_fusion.4), channel_id=1, source_target_pairs={{16,0},{32,16},{48,32},{64,48},{80,64},{96,80},{112,96},{128,112},... | collective-permute-start | bytes 49160 | tf_op jit(solution)/shard_map/while/body/eval_jaxpr/ppermute | solution.py:26
  131.4 6.8 %collective-permute-start = (f32[16,256]{1,0:T(8,128)S(1)}, f32[16,256]{1,0:T(8,128)S(1)}, u32[]{:S(2)}, u32[]{:S(2)}) collective-permute-start(f32[16,256]{1,0:T(8,128)S(1)} %multiply_add_fusion.4), channel_id=1, source_target_pairs={{16,0},{32,16},{48,32},{64,48},{80,64},{96,80},{112,96},{128,112},... | collective-permute-start | bytes 49160 | tf_op jit(solution)/shard_map/while/body/eval_jaxpr/ppermute | solution.py:26
  138.2 7.2 %collective-permute-start = (f32[16,256]{1,0:T(8,128)S(1)}, f32[16,256]{1,0:T(8,128)S(1)}, u32[]{:S(2)}, u32[]{:S(2)}) collective-permute-start(f32[16,256]{1,0:T(8,128)S(1)} %multiply_add_fusion.4), channel_id=1, source_target_pairs={{16,0},{32,16},{48,32},{64,48},{80,64},{96,80},{112,96},{128,112},... | collective-permute-start | bytes 49160 | tf_op jit(solution)/shard_map/while/body/eval_jaxpr/ppermute | solution.py:26
  145.4 7.2 %collective-permute-start = (f32[16,256]{1,0:T(8,128)S(1)}, f32[16,256]{1,0:T(8,128)S(1)}, u32[]{:S(2)}, u32[]{:S(2)}) collective-permute-start(f32[16,256]{1,0:T(8,128)S(1)} %multiply_add_fusion.4), channel_id=1, source_target_pairs={{16,0},{32,16},{48,32},{64,48},{80,64},{96,80},{112,96},{128,112},... | collective-permute-start | bytes 49160 | tf_op jit(solution)/shard_map/while/body/eval_jaxpr/ppermute | solution.py:26
  152.6 7.2 %collective-permute-start = (f32[16,256]{1,0:T(8,128)S(1)}, f32[16,256]{1,0:T(8,128)S(1)}, u32[]{:S(2)}, u32[]{:S(2)}) collective-permute-start(f32[16,256]{1,0:T(8,128)S(1)} %multiply_add_fusion.4), channel_id=1, source_target_pairs={{16,0},{32,16},{48,32},{64,48},{80,64},{96,80},{112,96},{128,112},... | collective-permute-start | bytes 49160 | tf_op jit(solution)/shard_map/while/body/eval_jaxpr/ppermute | solution.py:26
  159.7 7.2 %collective-permute-start = (f32[16,256]{1,0:T(8,128)S(1)}, f32[16,256]{1,0:T(8,128)S(1)}, u32[]{:S(2)}, u32[]{:S(2)}) collective-permute-start(f32[16,256]{1,0:T(8,128)S(1)} %multiply_add_fusion.4), channel_id=1, source_target_pairs={{16,0},{32,16},{48,32},{64,48},{80,64},{96,80},{112,96},{128,112},... | collective-permute-start | bytes 49160 | tf_op jit(solution)/shard_map/while/body/eval_jaxpr/ppermute | solution.py:26
  166.9 7.2 %collective-permute-start = (f32[16,256]{1,0:T(8,128)S(1)}, f32[16,256]{1,0:T(8,128)S(1)}, u32[]{:S(2)}, u32[]{:S(2)}) collective-permute-start(f32[16,256]{1,0:T(8,128)S(1)} %multiply_add_fusion.4), channel_id=1, source_target_pairs={{16,0},{32,16},{48,32},{64,48},{80,64},{96,80},{112,96},{128,112},... | collective-permute-start | bytes 49160 | tf_op jit(solution)/shard_map/while/body/eval_jaxpr/ppermute | solution.py:26
  179.3 7.2 %collective-permute-start.1 = (f32[3,2,256]{2,1,0:T(2,128)S(1)}, f32[3,2,256]{2,1,0:T(2,128)S(1)}, u32[]{:S(2)}, u32[]{:S(2)}) collective-permute-start(f32[3,2,256]{2,1,0:T(2,128)S(1)} %slice.53), channel_id=1, source_target_pairs={{16,0},{32,16},{48,32},{64,48},{80,64},{96,80},{112,96},{128,112},... | collective-permute-start | bytes 18440 | tf_op jit(solution)/shard_map/ppermute | solution.py:26
Sparse Core Ops, SparseCore 0:
  192.7 225.2 reduce-scatter.1
